TPU v7x, 256 devices: a whole 4x4x8 slice. The times are simulated.
256 devices in a mesh: ma: 32 (over x, z), row: 8 (over y, core).
Axes of the slice: x: 4, y: 4, z: 8, core: 2. Of those that a mesh axis runs over, the one named last changes fastest.
Arguments:
- grid_field: bfloat16 [512, 1536, 512], P(None, 'ma', 'row'), may hold values from -6 to 6
- legendre: bfloat16 [512, 1024, 1536], P(('ma', 'row')), may hold values from -0.15625 to 0.15625
- order_table: int32 [512], P(('ma', 'row')), may hold values from 0 to 1023, as said below
- boundary_rows: int32 [2, 2], replicated, may hold values from 96 to 127, as said below
- inverse: bfloat16 [1024, 256, 256], P(('ma', 'row')), may hold values from -0.375 to 0.375
Outputs:
- spectra: bfloat16 [1024, 256, 1024], P(('ma', 'row'))
Inputs may be any that keep to these rules, and one draw needn't show every extreme that they name: `order_table`: slots 2 i and 2 i + 1 hold the orders m and 1023 - m of one pair, m < 512 first; no order appears twice; the pair of 0 and 1023 is always present. `boundary_rows`: the four entries differ and lie in the top 128 // 4 Chebyshev rows; both ends of that range occur.
All inputs are finite; a program needn't handle non-finite values.
Results may differ from a plain program's by a relative error of at most 0.0049.
Values may be sent and summed in bfloat16 or wider, within the bound.
No kernel may reach another device: no remote copies, remote signals or barrier semaphores. Data moves between devices by JAX's collectives and lax.ppermute only.
A program may use at most 192 MiB of HBM per device.

v0:
```python
import jax
import jax.numpy as jnp
from jax import lax
from jax.sharding import PartitionSpec as P

NR = 128


def chebyshev_table(radial_levels):
    wave_number = jnp.arange(radial_levels, dtype=jnp.float32)[:, None]
    grid_point = jnp.arange(radial_levels, dtype=jnp.float32)[None, :]
    cos_table = jnp.cos(jnp.pi * wave_number * (grid_point + 0.5) / radial_levels) * jnp.sqrt(
        2.0 / radial_levels
    )
    return jnp.where(wave_number == 0.0, cos_table * jnp.sqrt(0.5), cos_table)


def boundary_keep(boundary_rows, radial_levels):
    row_index = jnp.arange(radial_levels, dtype=jnp.int32)[None, :]
    boundary_hit = (row_index == boundary_rows[:, 0:1]) | (row_index == boundary_rows[:, 1:2])
    return jnp.where(boundary_hit, 0.0, 1.0).astype(jnp.float32)


def on_device(grid_field, legendre, order_table, boundary_rows, inverse):
    ma_count = lax.axis_size("ma")
    row_count = lax.axis_size("row")
    degree_total = legendre.shape[1]
    radial_levels = NR
    degree_share = degree_total // (ma_count * row_count)
    finished_output = lax.all_to_all(
        lax.all_to_all(grid_field, "ma", split_axis=0, concat_axis=1, tiled=True),
        "row",
        split_axis=0,
        concat_axis=2,
        tiled=True,
    )
    spectral_coefficients = jnp.einsum(
        "xso,xod->xsd", legendre, finished_output, preferred_element_type=jnp.float32
    )
    degrees = jnp.arange(degree_total, dtype=jnp.int32)
    lower_mask = degrees[None, :] >= order_table[:, None]
    spectral_coefficients = jnp.where(
        lower_mask[:, :, None], spectral_coefficients, jnp.zeros_like(spectral_coefficients)
    )
    chebyshev = chebyshev_table(radial_levels)
    keep_rows = boundary_keep(boundary_rows, radial_levels)
    regrouped = lax.all_to_all(
        lax.all_to_all(spectral_coefficients, "ma", split_axis=1, concat_axis=0, tiled=True),
        "row",
        split_axis=1,
        concat_axis=0,
        tiled=True,
    )
    regrouped = regrouped.reshape(row_count, ma_count, 2, degree_share, radial_levels, 2, 2)
    coefficients = jnp.einsum(
        "kj,bavljqp->lqkabvp", chebyshev, regrouped, precision=lax.Precision.HIGHEST
    )
    right_side = coefficients * keep_rows[None, :, :, None, None, None, None]
    right_side = right_side.reshape(degree_share, 2 * radial_levels, -1).astype(jnp.bfloat16)
    solved = jnp.einsum("lij,ljn->lin", inverse, right_side, preferred_element_type=jnp.float32)
    return solved.astype(jnp.bfloat16)


def solution(mesh):
    return jax.shard_map(
        on_device,
        mesh=mesh,
        in_specs=(
            P(None, "ma", "row"),
            P(("ma", "row"), None, None),
            P(("ma", "row")),
            P(),
            P(("ma", "row"), None, None),
        ),
        out_specs=P(("ma", "row"), None, None),
        check_vma=False,
    )
```

profile of v0, /device:TPU:1, one launch (start us, length us, event | category | flops | bytes accessed | tf_op | source)
XLA Modules:
  0.0 457.8 jit_solution(13329561447722050809)
XLA Ops:
  0.0 8.7 %copy.26 = bf16[512,48,64]{2,1,0:T(8,128)(2,1)} copy(bf16[512,48,64]{0,2,1:T(8,128)(2,1)} %param.5) | data formatting | bytes 6291456 | tf_op args[0]
  8.7 8.8 %reshape.94 = bf16[32,2,24576]{2,1,0:T(2,128)(2,1)} reshape(bf16[512,48,64]{2,1,0:T(8,128)(2,1)} %copy.26) | data formatting | bytes 6291456
  17.4 81.5 %all_to_all.69 = bf16[32,2,24576]{2,1,0:T(2,128)(2,1)} all-to-all(bf16[32,2,24576]{2,1,0:T(2,128)(2,1)} %reshape.94), channel_id=1, replica_groups=mesh['ma'=32,'row'=8] {'ma'}, dimensions={0} | all-to-all | bytes 6291456 | tf_op jit(solution)/shard_map/all_to_all | solution.py:31
  99.0 8.8 %reshape.95 = bf16[512,48,64]{2,1,0:T(8,128)(2,1)} reshape(bf16[32,2,24576]{2,1,0:T(2,128)(2,1)} %all_to_all.69) | data formatting | bytes 6291456
  107.8 12.6 %copy.27 = bf16[16,32,48,64]{2,1,3,0:T(8,128)(2,1)} copy(bf16[16,32,48,64]{3,2,0,1:T(8,128)(2,1)} %bitcast.35) | data formatting | bytes 6291456 | tf_op jit(solution)/shard_map/all_to_all | solution.py:31
  120.4 15.7 %all_to_all.53 = bf16[16,1536,64]{1,2,0:T(8,128)(2,1)} reshape(bf16[16,32,48,64]{2,1,3,0:T(8,128)(2,1)} %copy.27) | data formatting | bytes 6291456 | tf_op jit(solution)/shard_map/all_to_all | solution.py:31
  136.1 9.6 %all-to-all-start.1 = ((bf16[16,1536,64]{1,2,0:T(8,128)(2,1)}), bf16[16,1536,64]{1,2,0:T(8,128)(2,1)}, u32[]{:S(2)}, u32[]{:S(2)}) async-start(bf16[16,1536,64]{1,2,0:T(8,128)(2,1)} %all_to_all.53), calls=%async_computation.1 | async-start | bytes 6291456 | tf_op jit(solution)/shard_map/all_to_all | solution.py:30
  145.7 37.6 %all-to-all-done.1 = bf16[16,1536,64]{1,2,0:T(8,128)(2,1)} async-done(((bf16[16,1536,64]{1,2,0:T(8,128)(2,1)}), bf16[16,1536,64]{1,2,0:T(8,128)(2,1)}, u32[]{:S(2)}, u32[]{:S(2)}) %all-to-all-start.1) | async-done | bytes 3145760 | tf_op jit(solution)/shard_map/all_to_all | solution.py:30
  183.3 2.2 copy.28
  185.5 5.6 %broadcast_select_fusion = f32[2,1024,512]{2,1,0:T(8,128)S(1)} fusion(pred[2,1024]{1,0:T(4,128)(4,1)S(1)} %iota_compare_fusion, bf16[2,1024,1536]{2,1,0:T(8,128)(2,1)} %param.6, bf16[2,1536,512]{1,2,0:T(8,128)(2,1)S(1)} %bitcast.38), kind=kOutput, calls=%fused_computation.2 | convolution fusion | flops 3222274048 | bytes 13633536 | tf_op jit(solution)/shard_map/xso,xod->xsd/dot_general | solution.py:37
  191.1 3.2 copy.30
  194.3 96.7 %all_to_all.70 = f32[2,1024,512]{2,0,1:T(2,128)S(1)} all-to-all(f32[2,1024,512]{2,0,1:T(2,128)S(1)} %copy.30), channel_id=1, replica_groups=mesh['ma'=32,'row'=8] {'ma'}, dimensions={1} | all-to-all | bytes 8388608 | tf_op jit(solution)/shard_map/all_to_all | solution.py:48
  291.0 0.8 copy.31
  291.8 0.8 copy.32
  292.6 4.4 copy.33
  297.0 9.6 %all-to-all-start.3 = ((f32[64,32,512]{2,0,1:T(8,128)}), f32[64,32,512]{2,0,1:T(8,128)}, u32[]{:S(2)}, u32[]{:S(2)}) async-start(f32[64,32,512]{2,0,1:T(8,128)} %copy.33), calls=%async_computation.3 | async-start | bytes 8388608 | tf_op jit(solution)/shard_map/all_to_all | solution.py:47
  306.9 48.6 %all-to-all-done.3 = f32[64,32,512]{2,0,1:T(8,128)} async-done(((f32[64,32,512]{2,0,1:T(8,128)}), f32[64,32,512]{2,0,1:T(8,128)}, u32[]{:S(2)}, u32[]{:S(2)}) %all-to-all-start.3) | async-done | bytes 4194336 | tf_op jit(solution)/shard_map/all_to_all | solution.py:47
  355.5 33.5 %copy.34 = f32[64,8,4,512]{1,3,2,0:T(8,128)} copy(f32[64,8,4,512]{3,0,2,1:T(8,128)} %bitcast.8) | data formatting | bytes 8388608 | tf_op jit(solution)/shard_map/all_to_all | solution.py:47
  389.0 53.4 %copy.35 = f32[8,32,2,4,128,2,2]{4,1,6,5,3,2,0:T(8,128)} copy(f32[8,32,2,4,128,2,2]{0,6,5,4,3,2,1:T(2,128)} %bitcast.10) | data formatting | bytes 8388608 | tf_op jit(solution)/shard_map/reshape | solution.py:54
  442.4 5.8 %fusion = bf16[4,2,128,32,8,2,2]{2,3,6,1,0,5,4:T(8,128)(2,1)S(1)} fusion(f32[2,128]{1,0:T(2,128)S(1)} %or_select_fusion, f32[8,32,2,4,128,2,2]{4,1,6,5,3,2,0:T(8,128)} %copy.35, f32[128]{0:T(128)S(1)} %get-tuple-element.7, f32[128]{0:T(128)S(1)} %get-tuple-element.8, pred[128]{0:T(512)(128)(4,1)S(1)} %iota_compare_fusion.1), kind=kOutput, calls=%fused_computation.3 | convolution fusion | flops 1612791808 | bytes 6293632 | tf_op jit(solution)/shard_map/kj,bavljqp->lqkabvp/dot_general | solution.py:55
  448.3 2.2 copy.36
  450.4 2.6 convert_element_type.17
  453.1 2.3 convert_bitcast_fusion
  455.4 2.4 copy.37
  (11 shorter events, 0.3 us)
Async XLA Ops:
  0.0 453.1 %copy-start = (bf16[4,256,256]{2,1,0:T(8,128)(2,1)S(1)}, bf16[4,256,256]{2,1,0:T(8,128)(2,1)}, u32[]{:S(2)}) copy-start(bf16[4,256,256]{2,1,0:T(8,128)(2,1)} %param.9) | copy-start | bytes 1572868
  136.1 9.6 %copy-start.2 = (s32[2]{0:T(128)S(1)}, s32[2]{0:T(128)}, u32[]{:S(2)}) copy-start(s32[2]{0:T(128)} %param.7) | copy-start | bytes 28
  136.1 47.2 %all-to-all-start.1 = ((bf16[16,1536,64]{1,2,0:T(8,128)(2,1)}), bf16[16,1536,64]{1,2,0:T(8,128)(2,1)}, u32[]{:S(2)}, u32[]{:S(2)}) async-start(bf16[16,1536,64]{1,2,0:T(8,128)(2,1)} %all_to_all.53), calls=%async_computation.1 | async-start | bytes 6291456 | tf_op jit(solution)/shard_map/all_to_all | solution.py:30
  297.0 9.6 %copy-start.1 = (s32[2,2]{1,0:T(2,128)S(1)}, s32[2,2]{1,0:T(2,128)}, u32[]{:S(2)}) copy-start(s32[2,2]{1,0:T(2,128)} %param.8) | copy-start | bytes 52
  297.0 58.5 %all-to-all-start.3 = ((f32[64,32,512]{2,0,1:T(8,128)}), f32[64,32,512]{2,0,1:T(8,128)}, u32[]{:S(2)}, u32[]{:S(2)}) async-start(f32[64,32,512]{2,0,1:T(8,128)} %copy.33), calls=%async_computation.3 | async-start | bytes 8388608 | tf_op jit(solution)/shard_map/all_to_all | solution.py:47
where the time goes:
time: 461 us; the launch traced here: 458 us
  blocking collectives  178 us (39%)
  local copies, waits for them, and re-layouts  160 us (35%)
  waiting for transfers between devices  86.2 us (19%)
  starting transfers between devices  19.1 us (4%)
  matrix products  13.7 us (3%)
    all_to_all x1, blocking collectives, on_device(): lax.all_to_all(spectral_coefficients, 'ma', split_axis=1, concat_axis=0,...  96.7 us
    all_to_all x1, blocking collectives, on_device(): lax.all_to_all(grid_field, 'ma', split_axis=0, concat_axis=1, tiled=True)  81.5 us
    reshape x1, local copies, waits for them, and re-layouts, on_device(): regrouped.reshape(row_count, ma_count, 2, degree_share, radial_levels, 2, 2)  53.4 us
    all_to_all x1, waiting for transfers between devices, on_device(): lax.all_to_all(lax.all_to_all(spectral_coefficients, 'ma', split_axis=1,...  48.6 us
    all_to_all x1, waiting for transfers between devices, on_device(): lax.all_to_all(lax.all_to_all(grid_field, 'ma', split_axis=0, concat_axis...  37.6 us
    all_to_all x1, local copies, waits for them, and re-layouts, on_device(): lax.all_to_all(lax.all_to_all(spectral_coefficients, 'ma', split_axis=1,...  33.5 us
    all_to_all x2, local copies, waits for them, and re-layouts, on_device(): lax.all_to_all(grid_field, 'ma', split_axis=0, concat_axis=1, tiled=True)  28.3 us
    unnamed x9, local copies, waits for them, and re-layouts  26.2 us
  transfers between devices with their start and end apart: 2, of which 2 were waited for; matrix products, arithmetic and copies ran while one was open for 0% of the time, Pallas kernels for 0%

commit v1 on v0

v1 whole, which is shorter than its diff:
```python
import jax
import jax.numpy as jnp
import ml_dtypes
import numpy as np
from jax import lax
from jax.experimental import pallas as pl
from jax.experimental.pallas import tpu as pltpu
from jax.sharding import PartitionSpec as P

AXES = ("ma", "row")
NR = 128
COLS = 4 * NR
LAT_STEP = 8
ROW_BLOCK = 256
SRC_STEP = 64
SRC_PERM = 32
VMEM = 56 * 1024 * 1024


def dot_nt(a, b):
    return lax.dot_general(a, b, (((1,), (1,)), ((), ())), preferred_element_type=jnp.float32)


def dot(a, b):
    return jnp.dot(a, b, preferred_element_type=jnp.float32)


def slot_unzip_matrix():
    m = np.zeros((256, 256), np.float32)
    for d in range(128):
        for h in range(2):
            m[2 * d + h, 128 * h + d] = 1.0
    return m.astype(ml_dtypes.bfloat16)


def chebyshev_matrices():
    k = np.arange(NR, dtype=np.float64)[:, None]
    j = np.arange(NR, dtype=np.float64)[None, :]
    table = np.cos(np.pi * k * (j + 0.5) / NR) * np.sqrt(2.0 / NR)
    table[0] = np.sqrt(1.0 / NR)
    full = np.zeros((COLS, COLS), np.float64)
    for p in range(2):
        for q in range(2):
            full[2 * q + p :: 4, 256 * p + 128 * q : 256 * p + 128 * q + 128] = table.T
    full = full.astype(np.float32)
    high = full.astype(ml_dtypes.bfloat16)
    low = (full - high.astype(np.float32)).astype(ml_dtypes.bfloat16)
    return high, low


def degree_gather_matrix():
    m = np.zeros((16 * SRC_PERM, 16 * SRC_PERM), np.float32)
    for p in range(2):
        for s in range(SRC_PERM):
            for h in range(2):
                for i in range(4):
                    m[((i * SRC_PERM + s) * 2 + h) * 2 + p, ((p * SRC_PERM + s) * 2 + h) * 4 + i] = 1.0
    return m.astype(ml_dtypes.bfloat16)


def pack_body(unzip_ref, x_ref, o_ref, f_ref):
    for g in range(2):
        x = x_ref[:, :, g * 256 : (g + 1) * 256].reshape(LAT_STEP * 64, 256)
        y = dot(x, unzip_ref[...])
        for t in range(LAT_STEP):
            rows = slice(t * 64, (t + 1) * 64)
            b = jnp.concatenate([y[rows, :128], y[rows, 128:]], axis=0)
            f_ref[pl.ds(g * 128 * LAT_STEP + t, 128, stride=LAT_STEP), :] = b.T
    o_ref[...] = f_ref[...].reshape(256, LAT_STEP, 128).astype(jnp.bfloat16)


def pack(grid_field):
    x = jnp.transpose(grid_field, (1, 2, 0))
    lat = x.shape[0]
    return pl.pallas_call(
        pack_body,
        name="pack",
        grid=(lat // LAT_STEP,),
        in_specs=[
            pl.BlockSpec((256, 256), lambda t: (0, 0)),
            pl.BlockSpec((LAT_STEP, 64, 512), lambda t: (t, 0, 0)),
        ],
        out_specs=pl.BlockSpec((256, LAT_STEP, 128), lambda t: (0, t, 0)),
        out_shape=jax.ShapeDtypeStruct((256, lat, 128), jnp.bfloat16),
        scratch_shapes=[pltpu.VMEM((256 * LAT_STEP, 128), jnp.float32)],
        compiler_params=pltpu.CompilerParams(vmem_limit_bytes=VMEM),
    )(jnp.asarray(slot_unzip_matrix()), x)


def analysis_body(order_ref, recv_ref, low_leg_ref, high_leg_ref, chi_ref, clo_ref, keep_ref, o_ref, f_ref):
    step = pl.program_id(0)

    @pl.when(step == 0)
    def _():
        lane = lax.broadcasted_iota(jnp.int32, (48, 128), 1)
        for a in range(32):
            for y in range(4):
                u = recv_ref[a * 8 + 2 * y]
                v = recv_ref[a * 8 + 2 * y + 1]
                ur = jnp.concatenate([u[:, 64:], u[:, :64]], axis=1)
                vr = jnp.concatenate([v[:, 64:], v[:, :64]], axis=1)
                f_ref[0, a * 48 : (a + 1) * 48, y * 128 : (y + 1) * 128] = jnp.where(lane < 64, u, vr)
                f_ref[1, a * 48 : (a + 1) * 48, y * 128 : (y + 1) * 128] = jnp.where(lane < 64, ur, v)

    degree = step * ROW_BLOCK + lax.broadcasted_iota(jnp.int32, (ROW_BLOCK, COLS), 0)

    def transform(leg, h):
        s = dot(leg, f_ref[h])
        s = jnp.where(degree >= order_ref[h], s, 0.0)
        hi = s.astype(jnp.bfloat16)
        lo = (s - hi.astype(jnp.float32)).astype(jnp.bfloat16)
        c = dot(hi, clo_ref[...]) + dot(lo, chi_ref[...]) + dot(hi, chi_ref[...])
        return (c * keep_ref[...]).reshape(ROW_BLOCK // 8, 8, COLS)

    sub = lax.broadcasted_iota(jnp.int32, (ROW_BLOCK // 8, 8, COLS), 1)

    def store(a, b):
        even = jnp.where(sub < 4, a, pltpu.roll(b, 4, 1))
        odd = jnp.where(sub < 4, pltpu.roll(a, 4, 1), b)
        both = jnp.stack([even, odd], axis=1).reshape(ROW_BLOCK // 4, 8, COLS)
        o_ref[...] = both.astype(jnp.bfloat16)

    @pl.when(step < 512 // ROW_BLOCK)
    def _():
        a = transform(low_leg_ref[0], 0)
        store(a, jnp.zeros_like(a))

    @pl.when(step >= 512 // ROW_BLOCK)
    def _():
        store(transform(low_leg_ref[0], 0), transform(high_leg_ref[0], 1))


def analysis(order_table, recv, legendre, keep):
    chi, clo = chebyshev_matrices()
    whole = lambda *shape: pl.BlockSpec(shape, lambda b: (0,) * len(shape))
    half = 512 // ROW_BLOCK
    return pl.pallas_call(
        analysis_body,
        name="analysis",
        grid=(1024 // ROW_BLOCK,),
        in_specs=[
            pl.BlockSpec(memory_space=pltpu.SMEM),
            whole(256, 48, 128),
            pl.BlockSpec((1, ROW_BLOCK, 1536), lambda b: (0, b, 0)),
            pl.BlockSpec((1, ROW_BLOCK, 1536), lambda b: (1, jnp.maximum(b, half), 0)),
            whole(COLS, COLS),
            whole(COLS, COLS),
            whole(1, COLS),
        ],
        out_specs=pl.BlockSpec((ROW_BLOCK // 4, 8, COLS), lambda b: (b, 0, 0)),
        out_shape=jax.ShapeDtypeStruct((256, 8, COLS), jnp.bfloat16),
        scratch_shapes=[pltpu.VMEM((2, 1536, COLS), jnp.bfloat16)],
        compiler_params=pltpu.CompilerParams(vmem_limit_bytes=VMEM),
    )(order_table, recv, legendre, legendre, jnp.asarray(chi), jnp.asarray(clo), keep)


def solve_body(gather_ref, recv_ref, inverse_ref, o_ref):
    parts = []
    for s in range(SRC_STEP // SRC_PERM):
        block = recv_ref[s * SRC_PERM : (s + 1) * SRC_PERM].reshape(SRC_PERM * 8, COLS)
        rows = jnp.concatenate([block[:, :256], block[:, 256:]], axis=0)
        parts.append(dot(gather_ref[...], rows).astype(jnp.bfloat16))
    per = 4 * SRC_PERM
    for i in range(4):
        r = jnp.concatenate([part[i * per : (i + 1) * per] for part in parts], axis=0)
        o_ref[i] = dot_nt(inverse_ref[i], r).astype(jnp.bfloat16)


def solve(recv, inverse):
    whole = lambda *shape: pl.BlockSpec(shape, lambda b: (0,) * len(shape))
    return pl.pallas_call(
        solve_body,
        name="solve",
        grid=(256 // SRC_STEP,),
        in_specs=[
            whole(16 * SRC_PERM, 16 * SRC_PERM),
            pl.BlockSpec((SRC_STEP, 8, COLS), lambda b: (b, 0, 0)),
            whole(4, 256, 256),
        ],
        out_specs=pl.BlockSpec((4, 256, 4 * SRC_STEP), lambda b: (0, 0, b)),
        out_shape=jax.ShapeDtypeStruct((4, 256, 1024), jnp.bfloat16),
        compiler_params=pltpu.CompilerParams(vmem_limit_bytes=VMEM),
    )(jnp.asarray(degree_gather_matrix()), recv, inverse)


def keep_columns(boundary_rows):
    k = jnp.arange(NR, dtype=jnp.int32)[None, :]
    hit = (k == boundary_rows[:, 0:1]) | (k == boundary_rows[:, 1:2])
    keep = jnp.where(hit, 0.0, 1.0).astype(jnp.float32).reshape(1, 2 * NR)
    return jnp.concatenate([keep, keep], axis=1)


def exchange(x):
    return lax.all_to_all(x, AXES, split_axis=0, concat_axis=0, tiled=True)


def on_device(grid_field, legendre, order_table, boundary_rows, inverse):
    keep = keep_columns(boundary_rows)
    field = exchange(pack(grid_field))
    right_side = exchange(analysis(order_table, field, legendre, keep))
    return solve(right_side, inverse)


def solution(mesh):
    return jax.shard_map(
        on_device,
        mesh=mesh,
        in_specs=(
            P(None, "ma", "row"),
            P(("ma", "row"), None, None),
            P(("ma", "row")),
            P(),
            P(("ma", "row"), None, None),
        ),
        out_specs=P(("ma", "row"), None, None),
        check_vma=False,
    )
```

time: 461 us -> 177 us (0.38)
  local copies, waits for them, and re-layouts: 160 us -> 1.84 us
  blocking collectives: 178 us -> 60.8 us
  Pallas kernels: 0 us -> 23.2 us
  matrix products: 13.7 us -> 0 us
  waiting for transfers between devices: 86.2 us -> 74.8 us
    all_to_all x2 -> x1, blocking collectives: 178 us -> 60.8 us  [exchange(): return lax.all_to_all(x, AXES, split_axis=0, concat_axis=0, tiled=True)]
    all_to_all x7 -> x0, local copies, waits for them, and re-layouts: 70 us -> none  [the longest x1 33.5 us: on_device(): lax.all_to_all(lax.all_to_all(spectral_coefficients, 'ma', split_axis=1,...]
    reshape x1 -> x0, local copies, waits for them, and re-layouts: 53.4 us -> none  [on_device(): regrouped.reshape(row_count, ma_count, 2, degree_share, radial_levels, 2, 2)]
    unnamed x9 -> x4, local copies, waits for them, and re-layouts: 26.2 us -> 1.67 us
    pallas_call x0 -> x3, Pallas kernels: none -> 23.2 us  [the longest x1 10.9 us: analysis(): pl.pallas_call(analysis_body, name='analysis', grid=(1024 // ROW_BLOCK,),...]
    dot_general x3 -> x0, matrix products: 13.7 us -> none  [the longest x1 5.83 us: on_device(): jnp.einsum('kj,bavljqp->lqkabvp', chebyshev, regrouped, precision=lax.Pre...]
    all_to_all x2 -> x1, waiting for transfers between devices: 86.2 us -> 74.8 us  [exchange(): return lax.all_to_all(x, AXES, split_axis=0, concat_axis=0, tiled=True)]
    convert_element_type x3 -> x0, local copies, waits for them, and re-layouts: 7.15 us -> none  [the longest x2 4.77 us: on_device(): right_side.reshape(degree_share, 2 * radial_levels, -1).astype(jnp.bfloat16)]
  transfers between devices with their start and end apart: 2 -> 1, of which waited for: 2 -> 1; matrix products, arithmetic and copies ran while one was open for 0% -> 0% of each run, Pallas kernels for 0% -> 0%
where the time goes in v1:
time: 177 us
  waiting for transfers between devices  74.8 us (42%)
  blocking collectives  60.8 us (34%)
  Pallas kernels  23.2 us (13%)
  starting transfers between devices  15.6 us (9%)
  local copies, waits for them, and re-layouts  1.84 us (1%)
    all_to_all x1, waiting for transfers between devices, exchange(): return lax.all_to_all(x, AXES, split_axis=0, concat_axis=0, tiled=True)  74.8 us
    all_to_all x1, blocking collectives, exchange(): return lax.all_to_all(x, AXES, split_axis=0, concat_axis=0, tiled=True)  60.8 us
    all_to_all x1, starting transfers between devices, exchange(): return lax.all_to_all(x, AXES, split_axis=0, concat_axis=0, tiled=True)  15.6 us
    pallas_call x1, Pallas kernels, analysis(): pl.pallas_call(analysis_body, name='analysis', grid=(1024 // ROW_BLOCK,),...  10.9 us
    pallas_call x1, Pallas kernels, pack(): pl.pallas_call(pack_body, name='pack', grid=(lat // LAT_STEP,), in_specs=...  6.85 us
    pallas_call x1, Pallas kernels, solve(): pl.pallas_call(solve_body, name='solve', grid=(256 // SRC_STEP,), in_spec...  5.45 us
  transfers between devices with their start and end apart: 1, of which 1 were waited for; matrix products, arithmetic and copies ran while one was open for 0% of the time, Pallas kernels for 0%

profile of v1, /device:TPU:1, one launch (start us, length us, event | category | flops | bytes accessed | tf_op | source)
XLA Modules:
  0.0 176.9 jit_solution(842036011927342314)
XLA Ops:
  0.0 6.8 %pack.1 = bf16[256,48,128]{2,1,0:T(8,128)(2,1)} custom-call(bf16[256,256]{1,0:T(8,128)(2,1)} %constant.12.clone.unzip_ref, bf16[48,64,512]{2,1,0:T(8,128)(2,1)} %bitcast.2), custom_call_target="tpu_custom_call" | custom-call | tf_op jit(solution)/shard_map/pack/pallas_call | solution.py:75
  6.8 0.0 copy-start.1
  6.8 15.6 %all-to-all-start = ((bf16[256,48,128]{2,1,0:T(8,128)(2,1)}), bf16[256,48,128]{2,1,0:T(8,128)(2,1)S(1)}, u32[]{:S(2)}, u32[]{:S(2)}) async-start(bf16[256,48,128]{2,1,0:T(8,128)(2,1)} %pack.1), calls=%async_computation | async-start | bytes 6291456 | tf_op jit(solution)/shard_map/all_to_all | solution.py:194
  22.5 0.0 copy-done.1
  22.5 0.2 slice_reduce_fusion.1
  22.7 0.1 or_select_fusion
  22.8 0.6 pad_maximum_fusion.keep_ref
  23.4 74.8 %all-to-all-done.recv_ref = bf16[256,48,128]{2,1,0:T(8,128)(2,1)S(1)} async-done(((bf16[256,48,128]{2,1,0:T(8,128)(2,1)}), bf16[256,48,128]{2,1,0:T(8,128)(2,1)S(1)}, u32[]{:S(2)}, u32[]{:S(2)}) %all-to-all-start) | async-done | bytes 3145760 | tf_op jit(solution)/shard_map/all_to_all | solution.py:194
  98.2 0.0 copy-start
  98.2 1.7 copy-done
  99.8 10.9 %analysis.1 = bf16[256,8,512]{2,1,0:T(8,128)(2,1)} custom-call(s32[2]{0:T(128)} %order_ref.1, bf16[256,48,128]{2,1,0:T(8,128)(2,1)} %copy-done, bf16[2,1024,1536]{2,1,0:T(8,128)(2,1)} %high_leg_ref.1, bf16[2,1024,1536]{2,1,0:T(8,128)(2,1)} %high_leg_ref.1, bf16[512,512]{1,0:T(8,128)(2,1)} %constant.13.clone.chi_ref, ...), custom_call_target="tpu_custom_call" | custom-call | tf_op jit(solution)/shard_map/analysis/pallas_call | solution.py:137
  110.7 60.8 %all_to_all.10.recv_ref = bf16[256,8,512]{2,1,0:T(8,128)(2,1)} all-to-all(bf16[256,8,512]{2,1,0:T(8,128)(2,1)} %analysis.1), channel_id=1, replica_groups=mesh['ma'=32,'row'=8] {'ma','row'}, dimensions={0} | all-to-all | bytes 4194304 | tf_op jit(solution)/shard_map/all_to_all | solution.py:194
  171.5 5.4 %solve.1 = bf16[4,256,1024]{2,1,0:T(8,128)(2,1)} custom-call(bf16[512,512]{1,0:T(8,128)(2,1)} %constant.15.clone.gather_ref, bf16[256,8,512]{2,1,0:T(8,128)(2,1)} %all_to_all.10.recv_ref, bf16[4,256,256]{2,1,0:T(8,128)(2,1)} %inverse_ref.1), custom_call_target="tpu_custom_call" | custom-call | tf_op jit(solution)/shard_map/solve/pallas_call | solution.py:171
Async XLA Ops:
  6.8 15.7 %copy-start.1 = (s32[2,2]{1,0:T(2,128)S(1)}, s32[2,2]{1,0:T(2,128)}, u32[]{:S(2)}) copy-start(s32[2,2]{1,0:T(2,128)} %param.12) | copy-start | bytes 52
  6.8 91.3 %all-to-all-start = ((bf16[256,48,128]{2,1,0:T(8,128)(2,1)}), bf16[256,48,128]{2,1,0:T(8,128)(2,1)S(1)}, u32[]{:S(2)}, u32[]{:S(2)}) async-start(bf16[256,48,128]{2,1,0:T(8,128)(2,1)} %pack.1), calls=%async_computation | async-start | bytes 6291456 | tf_op jit(solution)/shard_map/all_to_all | solution.py:194
  98.2 1.7 copy-start

commit v2 on v1

v2 whole, which is shorter than its diff:
```python
import jax
import jax.numpy as jnp
import ml_dtypes
import numpy as np
from jax import lax
from jax.experimental import pallas as pl
from jax.experimental.pallas import tpu as pltpu
from jax.sharding import PartitionSpec as P

AXES = ("ma", "row")
NR = 128
COLS = 4 * NR
LAT_STEP = 24
ROW_BLOCK = 256
SRC_STEP = 64
SRC_PERM = 32
MIB = 1024 * 1024


def dot_nt(a, b):
    return lax.dot_general(a, b, (((1,), (1,)), ((), ())), preferred_element_type=jnp.float32)


def dot(a, b):
    return jnp.dot(a, b, preferred_element_type=jnp.float32)


def chebyshev_matrices():
    k = np.arange(NR, dtype=np.float64)[:, None]
    j = np.arange(NR, dtype=np.float64)[None, :]
    table = np.cos(np.pi * k * (j + 0.5) / NR) * np.sqrt(2.0 / NR)
    table[0] = np.sqrt(1.0 / NR)
    full = np.zeros((COLS, COLS), np.float64)
    for p in range(2):
        for q in range(2):
            full[2 * q + p :: 4, 256 * p + 128 * q : 256 * p + 128 * q + 128] = table.T
    full = full.astype(np.float32)
    swapped = full.reshape(4, 2, 64, COLS)[:, ::-1].reshape(COLS, COLS)
    full = np.stack([full, swapped])
    high = full.astype(ml_dtypes.bfloat16)
    low = (full - high.astype(np.float32)).astype(ml_dtypes.bfloat16)
    return high, low


def degree_gather_matrix():
    m = np.zeros((16 * SRC_PERM, 16 * SRC_PERM), np.float32)
    for p in range(2):
        for s in range(SRC_PERM):
            for h in range(2):
                for i in range(4):
                    m[((i * SRC_PERM + s) * 2 + h) * 2 + p, ((p * SRC_PERM + s) * 2 + h) * 4 + i] = 1.0
    return m.astype(ml_dtypes.bfloat16)


def pack_body(core_ref, x_hbm, o_hbm, x_ref, f_ref, o_ref, in_sem, out_sem):
    chunks = x_hbm.shape[0] // LAT_STEP

    def fetch(i):
        part = pl.ds(i * LAT_STEP, LAT_STEP)
        return pltpu.make_async_copy(x_hbm.at[part], x_ref.at[part], in_sem.at[i])

    def flush(i):
        part = pl.ds(i * LAT_STEP, LAT_STEP)
        return pltpu.make_async_copy(o_ref.at[:, part, :], o_hbm.at[:, part, :], out_sem.at[i])

    for i in range(chunks):
        fetch(i).start()
    source = lax.broadcasted_iota(jnp.int32, (256, 256), 0)
    target = lax.broadcasted_iota(jnp.int32, (256, 256), 1)
    first = source == 2 * (target % 128) + target // 128
    second = source == 2 * (target % 128) + 1 - target // 128
    unzip = jnp.where(core_ref[0] == 0, first.astype(jnp.float32), second.astype(jnp.float32)).astype(jnp.bfloat16)
    for i in range(chunks):
        fetch(i).wait()
        for g in range(2):
            x = x_ref[i * LAT_STEP : (i + 1) * LAT_STEP, :, g * 256 : (g + 1) * 256]
            y = dot(x.reshape(LAT_STEP * 64, 256), unzip).astype(jnp.bfloat16)
            for t in range(LAT_STEP):
                rows = slice(t * 64, (t + 1) * 64)
                b = jnp.concatenate([y[rows, :128], y[rows, 128:]], axis=0)
                f_ref[i, pl.ds(g * 128 * LAT_STEP + t, 128, stride=LAT_STEP), :] = b.T.astype(jnp.float32)
        o_ref[:, i * LAT_STEP : (i + 1) * LAT_STEP, :] = f_ref[i].reshape(256, LAT_STEP, 128).astype(jnp.bfloat16)
        flush(i).start()
    for i in range(chunks):
        flush(i).wait()


def pack(grid_field, core):
    x = jnp.transpose(grid_field, (1, 2, 0))
    lat = x.shape[0]
    chunks = lat // LAT_STEP
    return pl.pallas_call(
        pack_body,
        name="pack",
        in_specs=[pl.BlockSpec(memory_space=pltpu.SMEM), pl.BlockSpec(memory_space=pltpu.HBM)],
        out_specs=pl.BlockSpec(memory_space=pltpu.HBM),
        out_shape=jax.ShapeDtypeStruct((256, lat, 128), jnp.bfloat16),
        scratch_shapes=[
            pltpu.VMEM(x.shape, jnp.bfloat16),
            pltpu.VMEM((chunks, 256 * LAT_STEP, 128), jnp.float32),
            pltpu.VMEM((256, lat, 128), jnp.bfloat16),
            pltpu.SemaphoreType.DMA((chunks,)),
            pltpu.SemaphoreType.DMA((chunks,)),
        ],
        compiler_params=pltpu.CompilerParams(vmem_limit_bytes=58 * MIB),
    )(core, x)


def analysis_body(order_ref, boundary_ref, recv_ref, leg_ref, chi_ref, clo_ref, o_ref, f_ref):
    column = lax.broadcasted_iota(jnp.int32, (1, COLS), 1)
    mode, second = column % NR, (column // NR) % 2 == 1
    keep = jnp.ones((1, COLS), jnp.float32)
    for e in range(2):
        keep = jnp.where(mode == jnp.where(second, boundary_ref[1, e], boundary_ref[0, e]), 0.0, keep)
    lane = lax.broadcasted_iota(jnp.int32, (48, 128), 1)
    for a in range(32):
        for y in range(4):
            u = recv_ref[a * 8 + 2 * y]
            v = recv_ref[a * 8 + 2 * y + 1]
            f_ref[0, a * 48 : (a + 1) * 48, y * 128 : (y + 1) * 128] = jnp.where(lane < 64, u, v)
            f_ref[1, a * 48 : (a + 1) * 48, y * 128 : (y + 1) * 128] = jnp.where(lane < 64, v, u)

    iota = lax.broadcasted_iota(jnp.int32, (ROW_BLOCK, COLS), 0)
    sub = lax.broadcasted_iota(jnp.int32, (ROW_BLOCK // 8, 8, COLS), 1)
    step = ROW_BLOCK // 4

    def transform(h, block):
        s = dot(leg_ref[h, block * ROW_BLOCK : (block + 1) * ROW_BLOCK], f_ref[h])
        s = jnp.where(iota + block * ROW_BLOCK >= order_ref[h], s, 0.0)
        hi = s.astype(jnp.bfloat16)
        lo = (s - hi.astype(jnp.float32)).astype(jnp.bfloat16)
        c = dot(hi, clo_ref[h]) + dot(lo, chi_ref[h]) + dot(hi, chi_ref[h])
        return (c * keep).reshape(ROW_BLOCK // 8, 8, COLS)

    def store(block, a, b):
        if b is None:
            even = jnp.where(sub < 4, a, 0.0)
            odd = jnp.where(sub < 4, pltpu.roll(a, 4, 1), 0.0)
        else:
            even = jnp.where(sub < 4, a, pltpu.roll(b, 4, 1))
            odd = jnp.where(sub < 4, pltpu.roll(a, 4, 1), b)
        both = jnp.stack([even, odd], axis=1).reshape(step, 8, COLS)
        o_ref[block * step : (block + 1) * step] = both.astype(jnp.bfloat16)

    for block in range(1024 // ROW_BLOCK):
        low, high = block * ROW_BLOCK, (block + 1) * ROW_BLOCK
        even_on = order_ref[0] < high
        odd_on = order_ref[1] < high

        @pl.when(jnp.logical_not(even_on))
        def _():
            o_ref[block * step : (block + 1) * step] = jnp.zeros((step, 8, COLS), jnp.bfloat16)

        @pl.when(jnp.logical_and(even_on, jnp.logical_not(odd_on)))
        def _():
            store(block, transform(0, block), None)

        if high > 512:

            @pl.when(odd_on)
            def _():
                store(block, transform(0, block), transform(1, block))


def analysis(order_table, boundary_rows, recv, legendre):
    chi, clo = chebyshev_matrices()
    smem = pl.BlockSpec(memory_space=pltpu.SMEM)
    vmem = pl.BlockSpec(memory_space=pltpu.VMEM)
    return pl.pallas_call(
        analysis_body,
        name="analysis",
        in_specs=[smem, smem, vmem, vmem, vmem, vmem],
        out_specs=vmem,
        out_shape=jax.ShapeDtypeStruct((256, 8, COLS), jnp.bfloat16),
        scratch_shapes=[pltpu.VMEM((2, 1536, COLS), jnp.bfloat16)],
        compiler_params=pltpu.CompilerParams(vmem_limit_bytes=24 * MIB),
    )(order_table, boundary_rows, recv, legendre, jnp.asarray(chi), jnp.asarray(clo))


def solve_body(gather_ref, recv_ref, inverse_ref, o_ref):
    parts = []
    first = pl.program_id(0) * SRC_STEP
    for s in range(SRC_STEP // SRC_PERM):
        block = recv_ref[pl.ds(first + s * SRC_PERM, SRC_PERM)].reshape(SRC_PERM * 8, COLS)
        rows = jnp.concatenate([block[:, :256], block[:, 256:]], axis=0)
        parts.append(dot(gather_ref[...], rows).astype(jnp.bfloat16))
    per = 4 * SRC_PERM
    for i in range(4):
        r = jnp.concatenate([part[i * per : (i + 1) * per] for part in parts], axis=0)
        o_ref[i] = dot_nt(inverse_ref[i], r).astype(jnp.bfloat16)


def solve(recv, inverse):
    vmem = pl.BlockSpec(memory_space=pltpu.VMEM)
    return pl.pallas_call(
        solve_body,
        name="solve",
        grid=(256 // SRC_STEP,),
        in_specs=[
            vmem,
            vmem,
            vmem,
        ],
        out_specs=pl.BlockSpec((4, 256, 4 * SRC_STEP), lambda b: (0, 0, b)),
        out_shape=jax.ShapeDtypeStruct((4, 256, 1024), jnp.bfloat16),
        compiler_params=pltpu.CompilerParams(vmem_limit_bytes=16 * MIB),
    )(jnp.asarray(degree_gather_matrix()), recv, inverse)


def exchange(x):
    return lax.all_to_all(x, AXES, split_axis=0, concat_axis=0, tiled=True)


def on_device(grid_field, legendre, order_table, boundary_rows, inverse):
    core = (lax.axis_index("row") % 2).astype(jnp.int32).reshape(1)
    field = exchange(pack(grid_field, core))
    right_side = exchange(analysis(order_table, boundary_rows, field, legendre))
    return solve(right_side, inverse)


def solution(mesh):
    return jax.shard_map(
        on_device,
        mesh=mesh,
        in_specs=(
            P(None, "ma", "row"),
            P(("ma", "row"), None, None),
            P(("ma", "row")),
            P(),
            P(("ma", "row"), None, None),
        ),
        out_specs=P(("ma", "row"), None, None),
        check_vma=False,
    )
```

time: 177 us -> 166 us (0.938)
  blocking collectives: 60.8 us -> 151 us
  waiting for transfers between devices: 74.8 us -> 0 us
  starting transfers between devices: 15.6 us -> 0 us
  Pallas kernels: 23.2 us -> 14.6 us
  local copies, waits for them, and re-layouts: 1.84 us -> 0.03 us
    all_to_all x1 -> x2, blocking collectives: 60.8 us -> 151 us  [exchange(): return lax.all_to_all(x, AXES, split_axis=0, concat_axis=0, tiled=True)]
    all_to_all x1 -> x0, waiting for transfers between devices: 74.8 us -> none  [exchange(): return lax.all_to_all(x, AXES, split_axis=0, concat_axis=0, tiled=True)]
    all_to_all x1 -> x0, starting transfers between devices: 15.6 us -> none  [exchange(): return lax.all_to_all(x, AXES, split_axis=0, concat_axis=0, tiled=True)]
    pallas_call x2, Pallas kernels: 17.7 us -> 11 us  [the longest x1 6.25 us: analysis(): pl.pallas_call(analysis_body, name='analysis', in_specs=[smem, smem, vmem...]
    pallas_call x1, Pallas kernels: 5.45 us -> 3.59 us  [solve(): pl.pallas_call(solve_body, name='solve', grid=(256 // SRC_STEP,), in_spec...]
  transfers between devices with their start and end apart: 1 -> 0, of which waited for: 1 -> 0; matrix products, arithmetic and copies ran while one was open for 0% -> 0% of each run, Pallas kernels for 0% -> 0%
where the time goes in v2:
time: 166 us
  blocking collectives  151 us (91%)
  Pallas kernels  14.6 us (9%)
    all_to_all x2, blocking collectives, exchange(): return lax.all_to_all(x, AXES, split_axis=0, concat_axis=0, tiled=True)  151 us
    pallas_call x1, Pallas kernels, analysis(): pl.pallas_call(analysis_body, name='analysis', in_specs=[smem, smem, vmem...  6.25 us
    pallas_call x1, Pallas kernels, pack(): pl.pallas_call(pack_body, name='pack', in_specs=[pl.BlockSpec(memory_spac...  4.72 us
    pallas_call x1, Pallas kernels, solve(): pl.pallas_call(solve_body, name='solve', grid=(256 // SRC_STEP,), in_spec...  3.59 us

profile of v2, /device:TPU:1, one launch (start us, length us, event | category | flops | bytes accessed | tf_op | source)
XLA Modules:
  0.0 165.8 jit_solution(1589568424993433658)
XLA Ops:
  0.0 0.0 copy-start.1
  0.0 0.0 copy-start.2
  0.0 0.0 copy-start.5
  0.0 0.0 copy-start.6
  0.0 4.7 %pack.1 = bf16[256,48,128]{2,1,0:T(8,128)(2,1)} custom-call(s32[1]{0:T(128)} %bitcast.core_ref, bf16[48,64,512]{2,1,0:T(8,128)(2,1)} %bitcast.2), custom_call_target="tpu_custom_call" | custom-call | tf_op jit(solution)/shard_map/pack/pallas_call | solution.py:92
  4.8 0.0 copy-start
  4.8 91.3 %all_to_all.10.recv_ref = bf16[256,48,128]{2,1,0:T(8,128)(2,1)S(1)} all-to-all(bf16[256,48,128]{2,1,0:T(8,128)(2,1)} %pack.1), channel_id=1, replica_groups=mesh['ma'=32,'row'=8] {'ma','row'}, dimensions={0} | all-to-all | bytes 6291456 | tf_op jit(solution)/shard_map/all_to_all | solution.py:211
  96.1 0.0 copy-done.1
  96.1 0.0 copy-done.2
  96.1 0.0 copy-done.5
  96.1 0.0 copy-done.6
  96.1 0.0 copy-done
  96.1 6.3 %analysis.1 = bf16[256,8,512]{2,1,0:T(8,128)(2,1)S(1)} custom-call(s32[2]{0:T(128)S(1)} %copy-done.6, s32[2,2]{1,0:T(2,128)S(1)} %copy-done.5, bf16[256,48,128]{2,1,0:T(8,128)(2,1)S(1)} %all_to_all.10.recv_ref, bf16[2,1024,1536]{2,1,0:T(8,128)(2,1)S(1)} %copy-done, bf16[2,512,512]{2,1,0:T(8,128)(2,1)S(1)} %copy-done.2, bf16[2,512,512]{2,1,0:T(8,128)(2,1)S(1)} %copy-done.1), custom_call_target="tpu_custom_call" | custom-call | tf_op jit(solution)/shard_map/analysis/pallas_call | solution.py:169
  102.4 0.0 copy-start.3
  102.4 0.0 copy-start.4
  102.4 59.8 %all_to_all.11.recv_ref = bf16[256,8,512]{2,1,0:T(8,128)(2,1)S(1)} all-to-all(bf16[256,8,512]{2,1,0:T(8,128)(2,1)S(1)} %analysis.1), channel_id=1, replica_groups=mesh['ma'=32,'row'=8] {'ma','row'}, dimensions={0} | all-to-all | bytes 4194304 | tf_op jit(solution)/shard_map/all_to_all | solution.py:211
  162.2 0.0 copy-done.3
  162.2 0.0 copy-done.4
  162.2 3.6 %solve.1 = bf16[4,256,1024]{2,1,0:T(8,128)(2,1)} custom-call(bf16[512,512]{1,0:T(8,128)(2,1)S(1)} %copy-done.4, bf16[256,8,512]{2,1,0:T(8,128)(2,1)S(1)} %all_to_all.11.recv_ref, bf16[4,256,256]{2,1,0:T(8,128)(2,1)S(1)} %copy-done.3), custom_call_target="tpu_custom_call" | custom-call | tf_op jit(solution)/shard_map/solve/pallas_call | solution.py:195
Async XLA Ops:
  0.0 96.1 %copy-start.1 = (bf16[2,512,512]{2,1,0:T(8,128)(2,1)S(1)}, bf16[2,512,512]{2,1,0:T(8,128)(2,1)}, u32[]{:S(2)}) copy-start(bf16[2,512,512]{2,1,0:T(8,128)(2,1)} %constant.24.clone.clo_ref) | copy-start | bytes 3145732
  0.0 96.1 %copy-start.2 = (bf16[2,512,512]{2,1,0:T(8,128)(2,1)S(1)}, bf16[2,512,512]{2,1,0:T(8,128)(2,1)}, u32[]{:S(2)}) copy-start(bf16[2,512,512]{2,1,0:T(8,128)(2,1)} %constant.23.clone.chi_ref) | copy-start | bytes 3145732
  0.0 96.1 %copy-start.5 = (s32[2,2]{1,0:T(2,128)S(1)}, s32[2,2]{1,0:T(2,128)}, u32[]{:S(2)}) copy-start(s32[2,2]{1,0:T(2,128)} %boundary_ref.1) | copy-start | bytes 52
  0.0 96.1 %copy-start.6 = (s32[2]{0:T(128)S(1)}, s32[2]{0:T(128)}, u32[]{:S(2)}) copy-start(s32[2]{0:T(128)} %order_ref.1) | copy-start | bytes 28
  4.8 91.4 %copy-start = (bf16[2,1024,1536]{2,1,0:T(8,128)(2,1)S(1)}, bf16[2,1024,1536]{2,1,0:T(8,128)(2,1)}, u32[]{:S(2)}) copy-start(bf16[2,1024,1536]{2,1,0:T(8,128)(2,1)} %leg_ref.1) | copy-start | bytes 18874372
  102.4 59.8 %copy-start.3 = (bf16[4,256,256]{2,1,0:T(8,128)(2,1)S(1)}, bf16[4,256,256]{2,1,0:T(8,128)(2,1)}, u32[]{:S(2)}) copy-start(bf16[4,256,256]{2,1,0:T(8,128)(2,1)} %inverse_ref.1) | copy-start | bytes 1572868
  102.4 59.8 %copy-start.4 = (bf16[512,512]{1,0:T(8,128)(2,1)S(1)}, bf16[512,512]{1,0:T(8,128)(2,1)}, u32[]{:S(2)}) copy-start(bf16[512,512]{1,0:T(8,128)(2,1)} %constant.25.clone.gather_ref) | copy-start | bytes 1572868

commit v3 on v2

--- a/solution.py
+++ b/solution.py
@@ -12,8 +12,8 @@
 COLS = 4 * NR
 LAT_STEP = 24
 ROW_BLOCK = 256
-SRC_STEP = 64
-SRC_PERM = 32
+SRC_STEP = 128
+SRC_PERM = 16
 MIB = 1024 * 1024
 
 
@@ -124,42 +124,41 @@
     sub = lax.broadcasted_iota(jnp.int32, (ROW_BLOCK // 8, 8, COLS), 1)
     step = ROW_BLOCK // 4
 
-    def transform(h, block):
-        s = dot(leg_ref[h, block * ROW_BLOCK : (block + 1) * ROW_BLOCK], f_ref[h])
-        s = jnp.where(iota + block * ROW_BLOCK >= order_ref[h], s, 0.0)
+    def spectrum(h, block, masked):
+        first = block * ROW_BLOCK
+        if not isinstance(block, int):
+            first = pl.multiple_of(first, ROW_BLOCK)
+        s = dot(leg_ref[h, pl.ds(first, ROW_BLOCK)], f_ref[h])
+        return jnp.where(iota + first >= order_ref[h], s, 0.0) if masked else s
+
+    def transform(h, s):
         hi = s.astype(jnp.bfloat16)
         lo = (s - hi.astype(jnp.float32)).astype(jnp.bfloat16)
         c = dot(hi, clo_ref[h]) + dot(lo, chi_ref[h]) + dot(hi, chi_ref[h])
         return (c * keep).reshape(ROW_BLOCK // 8, 8, COLS)
 
     def store(block, a, b):
-        if b is None:
-            even = jnp.where(sub < 4, a, 0.0)
-            odd = jnp.where(sub < 4, pltpu.roll(a, 4, 1), 0.0)
-        else:
-            even = jnp.where(sub < 4, a, pltpu.roll(b, 4, 1))
-            odd = jnp.where(sub < 4, pltpu.roll(a, 4, 1), b)
+        even = jnp.where(sub < 4, a, 0.0 if b is None else pltpu.roll(b, 4, 1))
+        odd = jnp.where(sub < 4, pltpu.roll(a, 4, 1), 0.0 if b is None else b)
         both = jnp.stack([even, odd], axis=1).reshape(step, 8, COLS)
         o_ref[block * step : (block + 1) * step] = both.astype(jnp.bfloat16)
 
-    for block in range(1024 // ROW_BLOCK):
-        low, high = block * ROW_BLOCK, (block + 1) * ROW_BLOCK
-        even_on = order_ref[0] < high
-        odd_on = order_ref[1] < high
-
-        @pl.when(jnp.logical_not(even_on))
-        def _():
-            o_ref[block * step : (block + 1) * step] = jnp.zeros((step, 8, COLS), jnp.bfloat16)
-
-        @pl.when(jnp.logical_and(even_on, jnp.logical_not(odd_on)))
-        def _():
-            store(block, transform(0, block), None)
-
-        if high > 512:
-
-            @pl.when(odd_on)
-            def _():
-                store(block, transform(0, block), transform(1, block))
+    low_order = order_ref[0] < ROW_BLOCK
+    h = jnp.where(low_order, 0, 1)
+    s0 = spectrum(h, jnp.where(low_order, 0, 2), True)
+    s1 = spectrum(0, 1, True)
+    either = transform(h, s0)
+    s2 = spectrum(0, 2, False)
+    store(0, jnp.where(low_order, either, 0.0), None)
+    c1 = transform(0, s1)
+    s3 = spectrum(0, 3, False)
+    store(1, c1, None)
+    c2 = transform(0, s2)
+    s4 = spectrum(1, 3, True)
+    store(2, c2, jnp.where(low_order, 0.0, either))
+    c3 = transform(0, s3)
+    c4 = transform(1, s4)
+    store(3, c3, c4)
 
 
 def analysis(order_table, boundary_rows, recv, legendre):
@@ -177,17 +176,27 @@
     )(order_table, boundary_rows, recv, legendre, jnp.asarray(chi), jnp.asarray(clo))
 
 
-def solve_body(gather_ref, recv_ref, inverse_ref, o_ref):
-    parts = []
-    first = pl.program_id(0) * SRC_STEP
-    for s in range(SRC_STEP // SRC_PERM):
-        block = recv_ref[pl.ds(first + s * SRC_PERM, SRC_PERM)].reshape(SRC_PERM * 8, COLS)
-        rows = jnp.concatenate([block[:, :256], block[:, 256:]], axis=0)
-        parts.append(dot(gather_ref[...], rows).astype(jnp.bfloat16))
+def solve_body(gather_ref, recv_ref, inverse_ref, o_hbm, o_ref, sem):
+    chunks = 256 // SRC_STEP
+    wide = 4 * SRC_STEP
+
+    def flush(c):
+        part = pl.ds(c * wide, wide)
+        return pltpu.make_async_copy(o_ref.at[:, :, part], o_hbm.at[:, :, part], sem.at[c])
+
     per = 4 * SRC_PERM
-    for i in range(4):
-        r = jnp.concatenate([part[i * per : (i + 1) * per] for part in parts], axis=0)
-        o_ref[i] = dot_nt(inverse_ref[i], r).astype(jnp.bfloat16)
+    for c in range(chunks):
+        parts = []
+        for first in range(c * SRC_STEP, (c + 1) * SRC_STEP, SRC_PERM):
+            block = recv_ref[first : first + SRC_PERM].reshape(SRC_PERM * 8, COLS)
+            rows = jnp.concatenate([block[:, :256], block[:, 256:]], axis=0)
+            parts.append(dot(gather_ref[...], rows).astype(jnp.bfloat16))
+        for i in range(4):
+            r = jnp.concatenate([part[i * per : (i + 1) * per] for part in parts], axis=0)
+            o_ref[i, :, c * wide : (c + 1) * wide] = dot_nt(inverse_ref[i], r).astype(jnp.bfloat16)
+        flush(c).start()
+    for c in range(chunks):
+        flush(c).wait()
 
 
 def solve(recv, inverse):
@@ -195,14 +204,13 @@
     return pl.pallas_call(
         solve_body,
         name="solve",
-        grid=(256 // SRC_STEP,),
-        in_specs=[
-            vmem,
-            vmem,
-            vmem,
+        in_specs=[vmem, vmem, vmem],
+        out_specs=pl.BlockSpec(memory_space=pltpu.HBM),
+        out_shape=jax.ShapeDtypeStruct((4, 256, 1024), jnp.bfloat16),
+        scratch_shapes=[
+            pltpu.VMEM((4, 256, 1024), jnp.bfloat16),
+            pltpu.SemaphoreType.DMA((256 // SRC_STEP,)),
         ],
-        out_specs=pl.BlockSpec((4, 256, 4 * SRC_STEP), lambda b: (0, 0, b)),
-        out_shape=jax.ShapeDtypeStruct((4, 256, 1024), jnp.bfloat16),
         compiler_params=pltpu.CompilerParams(vmem_limit_bytes=16 * MIB),
     )(jnp.asarray(degree_gather_matrix()), recv, inverse)
 

time: 166 us -> 164 us (0.988)
  Pallas kernels: 14.6 us -> 12.7 us
where the time goes in v3:
time: 164 us
  blocking collectives  151 us (92%)
  Pallas kernels  12.7 us (8%)
    all_to_all x2, blocking collectives, exchange(): return lax.all_to_all(x, AXES, split_axis=0, concat_axis=0, tiled=True)  151 us
    pallas_call x1, Pallas kernels, analysis(): pl.pallas_call(analysis_body, name='analysis', in_specs=[smem, smem, vmem...  5.54 us
    pallas_call x1, Pallas kernels, pack(): pl.pallas_call(pack_body, name='pack', in_specs=[pl.BlockSpec(memory_spac...  4.72 us

profile of v3, /device:TPU:1, one launch (start us, length us, event | category | flops | bytes accessed | tf_op | source)
XLA Modules:
  0.0 163.8 jit_solution(1575880069332282228)
XLA Ops:
  0.0 0.0 copy-start.1
  0.0 0.0 copy-start.2
  0.0 0.0 copy-start.5
  0.0 0.0 copy-start.6
  0.0 4.7 %pack.1 = bf16[256,48,128]{2,1,0:T(8,128)(2,1)} custom-call(s32[1]{0:T(128)} %bitcast.core_ref, bf16[48,64,512]{2,1,0:T(8,128)(2,1)} %bitcast.2), custom_call_target="tpu_custom_call" | custom-call | tf_op jit(solution)/shard_map/pack/pallas_call | solution.py:92
  4.8 0.0 copy-start
  4.8 91.3 %all_to_all.10.recv_ref = bf16[256,48,128]{2,1,0:T(8,128)(2,1)S(1)} all-to-all(bf16[256,48,128]{2,1,0:T(8,128)(2,1)} %pack.1), channel_id=1, replica_groups=mesh['ma'=32,'row'=8] {'ma','row'}, dimensions={0} | all-to-all | bytes 6291456 | tf_op jit(solution)/shard_map/all_to_all | solution.py:219
  96.1 0.0 copy-done.1
  96.1 0.0 copy-done.2
  96.1 0.0 copy-done.5
  96.1 0.0 copy-done.6
  96.1 0.0 copy-done
  96.1 5.5 %analysis.1 = bf16[256,8,512]{2,1,0:T(8,128)(2,1)S(1)} custom-call(s32[2]{0:T(128)S(1)} %copy-done.6, s32[2,2]{1,0:T(2,128)S(1)} %copy-done.5, bf16[256,48,128]{2,1,0:T(8,128)(2,1)S(1)} %all_to_all.10.recv_ref, bf16[2,1024,1536]{2,1,0:T(8,128)(2,1)S(1)} %copy-done, bf16[2,512,512]{2,1,0:T(8,128)(2,1)S(1)} %copy-done.2, bf16[2,512,512]{2,1,0:T(8,128)(2,1)S(1)} %copy-done.1), custom_call_target="tpu_custom_call" | custom-call | tf_op jit(solution)/shard_map/analysis/pallas_call | solution.py:168
  101.7 0.0 copy-start.3
  101.7 0.0 copy-start.4
  101.7 59.7 %all_to_all.11.recv_ref = bf16[256,8,512]{2,1,0:T(8,128)(2,1)S(1)} all-to-all(bf16[256,8,512]{2,1,0:T(8,128)(2,1)S(1)} %analysis.1), channel_id=1, replica_groups=mesh['ma'=32,'row'=8] {'ma','row'}, dimensions={0} | all-to-all | bytes 4194304 | tf_op jit(solution)/shard_map/all_to_all | solution.py:219
  161.4 0.0 copy-done.3
  161.4 0.0 copy-done.4
  161.4 2.4 %solve.1 = bf16[4,256,1024]{2,1,0:T(8,128)(2,1)} custom-call(bf16[256,256]{1,0:T(8,128)(2,1)S(1)} %copy-done.4, bf16[256,8,512]{2,1,0:T(8,128)(2,1)S(1)} %all_to_all.11.recv_ref, bf16[4,256,256]{2,1,0:T(8,128)(2,1)S(1)} %copy-done.3), custom_call_target="tpu_custom_call" | custom-call | tf_op jit(solution)/shard_map/solve/pallas_call | solution.py:204
Async XLA Ops:
  0.0 96.1 %copy-start.1 = (bf16[2,512,512]{2,1,0:T(8,128)(2,1)S(1)}, bf16[2,512,512]{2,1,0:T(8,128)(2,1)}, u32[]{:S(2)}) copy-start(bf16[2,512,512]{2,1,0:T(8,128)(2,1)} %constant.24.clone.clo_ref) | copy-start | bytes 3145732
  0.0 96.1 %copy-start.2 = (bf16[2,512,512]{2,1,0:T(8,128)(2,1)S(1)}, bf16[2,512,512]{2,1,0:T(8,128)(2,1)}, u32[]{:S(2)}) copy-start(bf16[2,512,512]{2,1,0:T(8,128)(2,1)} %constant.23.clone.chi_ref) | copy-start | bytes 3145732
  0.0 96.1 %copy-start.5 = (s32[2,2]{1,0:T(2,128)S(1)}, s32[2,2]{1,0:T(2,128)}, u32[]{:S(2)}) copy-start(s32[2,2]{1,0:T(2,128)} %boundary_ref.1) | copy-start | bytes 52
  0.0 96.1 %copy-start.6 = (s32[2]{0:T(128)S(1)}, s32[2]{0:T(128)}, u32[]{:S(2)}) copy-start(s32[2]{0:T(128)} %order_ref.1) | copy-start | bytes 28
  4.8 91.4 %copy-start = (bf16[2,1024,1536]{2,1,0:T(8,128)(2,1)S(1)}, bf16[2,1024,1536]{2,1,0:T(8,128)(2,1)}, u32[]{:S(2)}) copy-start(bf16[2,1024,1536]{2,1,0:T(8,128)(2,1)} %leg_ref.1) | copy-start | bytes 18874372
  101.7 59.7 %copy-start.3 = (bf16[4,256,256]{2,1,0:T(8,128)(2,1)S(1)}, bf16[4,256,256]{2,1,0:T(8,128)(2,1)}, u32[]{:S(2)}) copy-start(bf16[4,256,256]{2,1,0:T(8,128)(2,1)} %inverse_ref.1) | copy-start | bytes 1572868
  101.7 59.7 %copy-start.4 = (bf16[256,256]{1,0:T(8,128)(2,1)S(1)}, bf16[256,256]{1,0:T(8,128)(2,1)}, u32[]{:S(2)}) copy-start(bf16[256,256]{1,0:T(8,128)(2,1)} %constant.25.clone.gather_ref) | copy-start | bytes 393220

commit v4 on v3

--- a/solution.py
+++ b/solution.py
@@ -10,7 +10,8 @@
 AXES = ("ma", "row")
 NR = 128
 COLS = 4 * NR
-LAT_STEP = 24
+LAT_CHUNKS = (16, 24, 8)
+LAT_PITCH = 24
 ROW_BLOCK = 256
 SRC_STEP = 128
 SRC_PERM = 16
@@ -53,42 +54,42 @@
 
 
 def pack_body(core_ref, x_hbm, o_hbm, x_ref, f_ref, o_ref, in_sem, out_sem):
-    chunks = x_hbm.shape[0] // LAT_STEP
+    starts = [sum(LAT_CHUNKS[:i]) for i in range(len(LAT_CHUNKS))]
+    parts = [pl.ds(first, size) for first, size in zip(starts, LAT_CHUNKS)]
 
     def fetch(i):
-        part = pl.ds(i * LAT_STEP, LAT_STEP)
-        return pltpu.make_async_copy(x_hbm.at[part], x_ref.at[part], in_sem.at[i])
+        return pltpu.make_async_copy(x_hbm.at[parts[i]], x_ref.at[parts[i]], in_sem.at[i])
 
     def flush(i):
-        part = pl.ds(i * LAT_STEP, LAT_STEP)
-        return pltpu.make_async_copy(o_ref.at[:, part, :], o_hbm.at[:, part, :], out_sem.at[i])
-
-    for i in range(chunks):
+        return pltpu.make_async_copy(o_ref.at[:, parts[i], :], o_hbm.at[:, parts[i], :], out_sem.at[i])
+
+    for i in range(len(parts)):
         fetch(i).start()
     source = lax.broadcasted_iota(jnp.int32, (256, 256), 0)
     target = lax.broadcasted_iota(jnp.int32, (256, 256), 1)
     first = source == 2 * (target % 128) + target // 128
     second = source == 2 * (target % 128) + 1 - target // 128
     unzip = jnp.where(core_ref[0] == 0, first.astype(jnp.float32), second.astype(jnp.float32)).astype(jnp.bfloat16)
-    for i in range(chunks):
+    for i, (start, size) in enumerate(zip(starts, LAT_CHUNKS)):
+        lat = slice(start, start + size)
         fetch(i).wait()
         for g in range(2):
-            x = x_ref[i * LAT_STEP : (i + 1) * LAT_STEP, :, g * 256 : (g + 1) * 256]
-            y = dot(x.reshape(LAT_STEP * 64, 256), unzip).astype(jnp.bfloat16)
-            for t in range(LAT_STEP):
+            x = x_ref[lat, :, g * 256 : (g + 1) * 256].reshape(size * 64, 256)
+            y = dot(x, unzip).astype(jnp.bfloat16)
+            for t in range(size):
                 rows = slice(t * 64, (t + 1) * 64)
                 b = jnp.concatenate([y[rows, :128], y[rows, 128:]], axis=0)
-                f_ref[i, pl.ds(g * 128 * LAT_STEP + t, 128, stride=LAT_STEP), :] = b.T.astype(jnp.float32)
-        o_ref[:, i * LAT_STEP : (i + 1) * LAT_STEP, :] = f_ref[i].reshape(256, LAT_STEP, 128).astype(jnp.bfloat16)
+                f_ref[i, pl.ds(g * 128 * LAT_PITCH + t, 128, stride=LAT_PITCH), :] = b.T.astype(jnp.float32)
+        o_ref[:, lat, :] = f_ref[i].reshape(256, LAT_PITCH, 128)[:, :size].astype(jnp.bfloat16)
         flush(i).start()
-    for i in range(chunks):
+    for i in range(len(parts)):
         flush(i).wait()
 
 
 def pack(grid_field, core):
     x = jnp.transpose(grid_field, (1, 2, 0))
     lat = x.shape[0]
-    chunks = lat // LAT_STEP
+    chunks = len(LAT_CHUNKS)
     return pl.pallas_call(
         pack_body,
         name="pack",
@@ -97,7 +98,7 @@
         out_shape=jax.ShapeDtypeStruct((256, lat, 128), jnp.bfloat16),
         scratch_shapes=[
             pltpu.VMEM(x.shape, jnp.bfloat16),
-            pltpu.VMEM((chunks, 256 * LAT_STEP, 128), jnp.float32),
+            pltpu.VMEM((chunks, 256 * LAT_PITCH, 128), jnp.float32),
             pltpu.VMEM((256, lat, 128), jnp.bfloat16),
             pltpu.SemaphoreType.DMA((chunks,)),
             pltpu.SemaphoreType.DMA((chunks,)),

time: 164 us -> 164 us (level)
  no operation moved by 1% of the time
where the time goes in v4:
time: 164 us
  blocking collectives  151 us (92%)
  Pallas kernels  12.4 us (8%)
    all_to_all x2, blocking collectives, exchange(): return lax.all_to_all(x, AXES, split_axis=0, concat_axis=0, tiled=True)  151 us
    pallas_call x1, Pallas kernels, analysis(): pl.pallas_call(analysis_body, name='analysis', in_specs=[smem, smem, vmem...  5.57 us
    pallas_call x1, Pallas kernels, pack(): pl.pallas_call(pack_body, name='pack', in_specs=[pl.BlockSpec(memory_spac...  4.47 us

profile of v4, /device:TPU:1, one launch (start us, length us, event | category | flops | bytes accessed | tf_op | source)
XLA Modules:
  0.0 163.5 jit_solution(5996585216754853863)
XLA Ops:
  0.0 0.0 copy-start.1
  0.0 0.0 copy-start.2
  0.0 0.0 copy-start.5
  0.0 0.0 copy-start.6
  0.0 4.5 %pack.1 = bf16[256,48,128]{2,1,0:T(8,128)(2,1)} custom-call(s32[1]{0:T(128)} %bitcast.core_ref, bf16[48,64,512]{2,1,0:T(8,128)(2,1)} %bitcast.2), custom_call_target="tpu_custom_call" | custom-call | tf_op jit(solution)/shard_map/pack/pallas_call | solution.py:93
  4.5 0.0 copy-start
  4.5 91.3 %all_to_all.10.recv_ref = bf16[256,48,128]{2,1,0:T(8,128)(2,1)S(1)} all-to-all(bf16[256,48,128]{2,1,0:T(8,128)(2,1)} %pack.1), channel_id=1, replica_groups=mesh['ma'=32,'row'=8] {'ma','row'}, dimensions={0} | all-to-all | bytes 6291456 | tf_op jit(solution)/shard_map/all_to_all | solution.py:220
  95.8 0.0 copy-done.1
  95.8 0.0 copy-done.2
  95.8 0.0 copy-done.5
  95.8 0.0 copy-done.6
  95.8 0.0 copy-done
  95.9 5.6 %analysis.1 = bf16[256,8,512]{2,1,0:T(8,128)(2,1)S(1)} custom-call(s32[2]{0:T(128)S(1)} %copy-done.6, s32[2,2]{1,0:T(2,128)S(1)} %copy-done.5, bf16[256,48,128]{2,1,0:T(8,128)(2,1)S(1)} %all_to_all.10.recv_ref, bf16[2,1024,1536]{2,1,0:T(8,128)(2,1)S(1)} %copy-done, bf16[2,512,512]{2,1,0:T(8,128)(2,1)S(1)} %copy-done.2, bf16[2,512,512]{2,1,0:T(8,128)(2,1)S(1)} %copy-done.1), custom_call_target="tpu_custom_call" | custom-call | tf_op jit(solution)/shard_map/analysis/pallas_call | solution.py:169
  101.4 0.0 copy-start.3
  101.4 0.0 copy-start.4
  101.5 59.6 %all_to_all.11.recv_ref = bf16[256,8,512]{2,1,0:T(8,128)(2,1)S(1)} all-to-all(bf16[256,8,512]{2,1,0:T(8,128)(2,1)S(1)} %analysis.1), channel_id=1, replica_groups=mesh['ma'=32,'row'=8] {'ma','row'}, dimensions={0} | all-to-all | bytes 4194304 | tf_op jit(solution)/shard_map/all_to_all | solution.py:220
  161.1 0.0 copy-done.3
  161.1 0.0 copy-done.4
  161.1 2.4 %solve.1 = bf16[4,256,1024]{2,1,0:T(8,128)(2,1)} custom-call(bf16[256,256]{1,0:T(8,128)(2,1)S(1)} %copy-done.4, bf16[256,8,512]{2,1,0:T(8,128)(2,1)S(1)} %all_to_all.11.recv_ref, bf16[4,256,256]{2,1,0:T(8,128)(2,1)S(1)} %copy-done.3), custom_call_target="tpu_custom_call" | custom-call | tf_op jit(solution)/shard_map/solve/pallas_call | solution.py:205
Async XLA Ops:
  0.0 95.8 %copy-start.1 = (bf16[2,512,512]{2,1,0:T(8,128)(2,1)S(1)}, bf16[2,512,512]{2,1,0:T(8,128)(2,1)}, u32[]{:S(2)}) copy-start(bf16[2,512,512]{2,1,0:T(8,128)(2,1)} %constant.24.clone.clo_ref) | copy-start | bytes 3145732
  0.0 95.8 %copy-start.2 = (bf16[2,512,512]{2,1,0:T(8,128)(2,1)S(1)}, bf16[2,512,512]{2,1,0:T(8,128)(2,1)}, u32[]{:S(2)}) copy-start(bf16[2,512,512]{2,1,0:T(8,128)(2,1)} %constant.23.clone.chi_ref) | copy-start | bytes 3145732
  0.0 95.8 %copy-start.5 = (s32[2,2]{1,0:T(2,128)S(1)}, s32[2,2]{1,0:T(2,128)}, u32[]{:S(2)}) copy-start(s32[2,2]{1,0:T(2,128)} %boundary_ref.1) | copy-start | bytes 52
  0.0 95.8 %copy-start.6 = (s32[2]{0:T(128)S(1)}, s32[2]{0:T(128)}, u32[]{:S(2)}) copy-start(s32[2]{0:T(128)} %order_ref.1) | copy-start | bytes 28
  4.5 91.3 %copy-start = (bf16[2,1024,1536]{2,1,0:T(8,128)(2,1)S(1)}, bf16[2,1024,1536]{2,1,0:T(8,128)(2,1)}, u32[]{:S(2)}) copy-start(bf16[2,1024,1536]{2,1,0:T(8,128)(2,1)} %leg_ref.1) | copy-start | bytes 18874372
  101.4 59.7 %copy-start.3 = (bf16[4,256,256]{2,1,0:T(8,128)(2,1)S(1)}, bf16[4,256,256]{2,1,0:T(8,128)(2,1)}, u32[]{:S(2)}) copy-start(bf16[4,256,256]{2,1,0:T(8,128)(2,1)} %inverse_ref.1) | copy-start | bytes 1572868
  101.4 59.7 %copy-start.4 = (bf16[256,256]{1,0:T(8,128)(2,1)S(1)}, bf16[256,256]{1,0:T(8,128)(2,1)}, u32[]{:S(2)}) copy-start(bf16[256,256]{1,0:T(8,128)(2,1)} %constant.25.clone.gather_ref) | copy-start | bytes 393220

commit v5 on v4

--- a/solution.py
+++ b/solution.py
@@ -181,9 +181,9 @@
     chunks = 256 // SRC_STEP
     wide = 4 * SRC_STEP
 
-    def flush(c):
+    def flush(c, i):
         part = pl.ds(c * wide, wide)
-        return pltpu.make_async_copy(o_ref.at[:, :, part], o_hbm.at[:, :, part], sem.at[c])
+        return pltpu.make_async_copy(o_ref.at[i, :, part], o_hbm.at[i, :, part], sem.at[c, i])
 
     per = 4 * SRC_PERM
     for c in range(chunks):
@@ -195,9 +195,10 @@
         for i in range(4):
             r = jnp.concatenate([part[i * per : (i + 1) * per] for part in parts], axis=0)
             o_ref[i, :, c * wide : (c + 1) * wide] = dot_nt(inverse_ref[i], r).astype(jnp.bfloat16)
-        flush(c).start()
+            flush(c, i).start()
     for c in range(chunks):
-        flush(c).wait()
+        for i in range(4):
+            flush(c, i).wait()
 
 
 def solve(recv, inverse):
@@ -210,7 +211,7 @@
         out_shape=jax.ShapeDtypeStruct((4, 256, 1024), jnp.bfloat16),
         scratch_shapes=[
             pltpu.VMEM((4, 256, 1024), jnp.bfloat16),
-            pltpu.SemaphoreType.DMA((256 // SRC_STEP,)),
+            pltpu.SemaphoreType.DMA((256 // SRC_STEP, 4)),
         ],
         compiler_params=pltpu.CompilerParams(vmem_limit_bytes=16 * MIB),
     )(jnp.asarray(degree_gather_matrix()), recv, inverse)

time: 164 us -> 164 us (level)
  no operation moved by 1% of the time
where the time goes in v5:
time: 164 us; the launch traced here: 163 us
  blocking collectives  151 us (92%)
  Pallas kernels  12.3 us (8%)
    all_to_all x2, blocking collectives, exchange(): return lax.all_to_all(x, AXES, split_axis=0, concat_axis=0, tiled=True)  151 us
    pallas_call x1, Pallas kernels, analysis(): pl.pallas_call(analysis_body, name='analysis', in_specs=[smem, smem, vmem...  5.54 us
    pallas_call x1, Pallas kernels, pack(): pl.pallas_call(pack_body, name='pack', in_specs=[pl.BlockSpec(memory_spac...  4.47 us

profile of v5, /device:TPU:1, one launch (start us, length us, event | category | flops | bytes accessed | tf_op | source)
XLA Modules:
  0.0 163.4 jit_solution(17130663507537133912)
XLA Ops:
  0.0 0.0 copy-start.1
  0.0 0.0 copy-start.2
  0.0 0.0 copy-start.5
  0.0 0.0 copy-start.6
  0.0 4.5 %pack.1 = bf16[256,48,128]{2,1,0:T(8,128)(2,1)} custom-call(s32[1]{0:T(128)} %bitcast.core_ref, bf16[48,64,512]{2,1,0:T(8,128)(2,1)} %bitcast.2), custom_call_target="tpu_custom_call" | custom-call | tf_op jit(solution)/shard_map/pack/pallas_call | solution.py:93
  4.5 0.0 copy-start
  4.5 91.3 %all_to_all.10.recv_ref = bf16[256,48,128]{2,1,0:T(8,128)(2,1)S(1)} all-to-all(bf16[256,48,128]{2,1,0:T(8,128)(2,1)} %pack.1), channel_id=1, replica_groups=mesh['ma'=32,'row'=8] {'ma','row'}, dimensions={0} | all-to-all | bytes 6291456 | tf_op jit(solution)/shard_map/all_to_all | solution.py:221
  95.8 0.0 copy-done.1
  95.8 0.0 copy-done.2
  95.8 0.0 copy-done.5
  95.8 0.0 copy-done.6
  95.8 0.0 copy-done
  95.9 5.5 %analysis.1 = bf16[256,8,512]{2,1,0:T(8,128)(2,1)S(1)} custom-call(s32[2]{0:T(128)S(1)} %copy-done.6, s32[2,2]{1,0:T(2,128)S(1)} %copy-done.5, bf16[256,48,128]{2,1,0:T(8,128)(2,1)S(1)} %all_to_all.10.recv_ref, bf16[2,1024,1536]{2,1,0:T(8,128)(2,1)S(1)} %copy-done, bf16[2,512,512]{2,1,0:T(8,128)(2,1)S(1)} %copy-done.2, bf16[2,512,512]{2,1,0:T(8,128)(2,1)S(1)} %copy-done.1), custom_call_target="tpu_custom_call" | custom-call | tf_op jit(solution)/shard_map/analysis/pallas_call | solution.py:169
  101.4 0.0 copy-start.3
  101.4 0.0 copy-start.4
  101.4 59.7 %all_to_all.11.recv_ref = bf16[256,8,512]{2,1,0:T(8,128)(2,1)S(1)} all-to-all(bf16[256,8,512]{2,1,0:T(8,128)(2,1)S(1)} %analysis.1), channel_id=1, replica_groups=mesh['ma'=32,'row'=8] {'ma','row'}, dimensions={0} | all-to-all | bytes 4194304 | tf_op jit(solution)/shard_map/all_to_all | solution.py:221
  161.1 0.0 copy-done.3
  161.1 0.0 copy-done.4
  161.1 2.3 %solve.1 = bf16[4,256,1024]{2,1,0:T(8,128)(2,1)} custom-call(bf16[256,256]{1,0:T(8,128)(2,1)S(1)} %copy-done.4, bf16[256,8,512]{2,1,0:T(8,128)(2,1)S(1)} %all_to_all.11.recv_ref, bf16[4,256,256]{2,1,0:T(8,128)(2,1)S(1)} %copy-done.3), custom_call_target="tpu_custom_call" | custom-call | tf_op jit(solution)/shard_map/solve/pallas_call | solution.py:206
Async XLA Ops:
  0.0 95.8 %copy-start.1 = (bf16[2,512,512]{2,1,0:T(8,128)(2,1)S(1)}, bf16[2,512,512]{2,1,0:T(8,128)(2,1)}, u32[]{:S(2)}) copy-start(bf16[2,512,512]{2,1,0:T(8,128)(2,1)} %constant.24.clone.clo_ref) | copy-start | bytes 3145732
  0.0 95.8 %copy-start.2 = (bf16[2,512,512]{2,1,0:T(8,128)(2,1)S(1)}, bf16[2,512,512]{2,1,0:T(8,128)(2,1)}, u32[]{:S(2)}) copy-start(bf16[2,512,512]{2,1,0:T(8,128)(2,1)} %constant.23.clone.chi_ref) | copy-start | bytes 3145732
  0.0 95.8 %copy-start.5 = (s32[2,2]{1,0:T(2,128)S(1)}, s32[2,2]{1,0:T(2,128)}, u32[]{:S(2)}) copy-start(s32[2,2]{1,0:T(2,128)} %boundary_ref.1) | copy-start | bytes 52
  0.0 95.8 %copy-start.6 = (s32[2]{0:T(128)S(1)}, s32[2]{0:T(128)}, u32[]{:S(2)}) copy-start(s32[2]{0:T(128)} %order_ref.1) | copy-start | bytes 28
  4.5 91.3 %copy-start = (bf16[2,1024,1536]{2,1,0:T(8,128)(2,1)S(1)}, bf16[2,1024,1536]{2,1,0:T(8,128)(2,1)}, u32[]{:S(2)}) copy-start(bf16[2,1024,1536]{2,1,0:T(8,128)(2,1)} %leg_ref.1) | copy-start | bytes 18874372
  101.4 59.7 %copy-start.3 = (bf16[4,256,256]{2,1,0:T(8,128)(2,1)S(1)}, bf16[4,256,256]{2,1,0:T(8,128)(2,1)}, u32[]{:S(2)}) copy-start(bf16[4,256,256]{2,1,0:T(8,128)(2,1)} %inverse_ref.1) | copy-start | bytes 1572868
  101.4 59.7 %copy-start.4 = (bf16[256,256]{1,0:T(8,128)(2,1)S(1)}, bf16[256,256]{1,0:T(8,128)(2,1)}, u32[]{:S(2)}) copy-start(bf16[256,256]{1,0:T(8,128)(2,1)} %constant.25.clone.gather_ref) | copy-start | bytes 393220
